TPU v7x, 32 devices: a whole 2x2x4 slice. The times are simulated.
32 devices in a mesh: rep: 8 (over z, y), tp: 4 (over x, core).
Axes of the slice: x: 2, y: 2, z: 4, core: 2. Of those that a mesh axis runs over, the one named last changes fastest.
Arguments:
- tokens: bfloat16 [8192, 8192], P('rep', 'tp'), may hold values from -6 to 6
- grad_out: bfloat16 [8192, 4096], P('rep', 'tp'), may hold values from -0.0625 to 0.0625
- lengths: int32 [8, 4], replicated, may hold values from 0 to 1024, as said below
- master: float32 [8192, 2048], P('rep', 'tp'), may hold values from -3 to 3
- first: float32 [8192, 2048], P('rep', 'tp'), may hold values from -6 to 6
- second: float32 [8192, 2048], P('rep', 'tp'), may hold values from 0.25 to 4
Outputs:
- new_master: float32 [8192, 2048], P('rep', 'tp')
- new_first: float32 [8192, 2048], P('rep', 'tp')
- new_second: float32 [8192, 2048], P('rep', 'tp')
- healthy_weights: bfloat16 [8192, 2048], P(None, 'tp')
- slot_weights: bfloat16 [8, 8192, 4096], P('rep', None, 'tp')
Inputs may be any that keep to these rules, and one draw needn't show every extreme that they name: `lengths`: each row is one replica's split of the 2048 columns over its devices in tp order: the entries are multiples of 256, sum to 2048, the nonzero ones come first and number at least half of the row; a row is either all 512 or has an entry equal to 1024, and some row has an entry equal to 1024.
All inputs are finite; a program needn't handle non-finite values.
Results may differ from a plain program's by a relative error of at most 0.0019.
Values may be sent and summed in bfloat16 or wider, within the bound.
A program may use at most 128 MiB of HBM per device.

v0:
```python
import jax
import jax.numpy as jnp
from jax import lax
from jax.sharding import PartitionSpec as P

COLS = 2048
STEP = 1000


decay_first = 0.9
decay_second = 0.999
learning_rate = 0.02
weight_decay = 0.1
epsilon = 1e-08


def adam_update(master, first, second, gradient):
    scale_first = 1.0 - decay_first**STEP
    scale_second = 1.0 - decay_second**STEP
    new_first = decay_first * first + (1.0 - decay_first) * gradient
    new_second = decay_second * second + (1.0 - decay_second) * gradient * gradient
    direction = new_first / scale_first / (jnp.sqrt(new_second / scale_second) + epsilon)
    new_master = master - learning_rate * (direction + weight_decay * master)
    return (new_master, new_first, new_second)


def on_device(tokens, grad_out, lengths, master, first, second):
    shards = lax.axis_size("tp")
    replicas = lax.axis_size("rep")
    column_index = lax.axis_index("tp")
    replica_index = lax.axis_index("rep")
    token_count = tokens.shape[0]
    slot_width = grad_out.shape[1]
    block_width = COLS // shards
    begins_all = jnp.cumsum(lengths, axis=1) - lengths
    is_mine = jnp.arange(shards, dtype=jnp.int32) == column_index
    own_lengths = lax.dynamic_index_in_dim(lengths, replica_index, 0, keepdims=False)
    own_begins = lax.dynamic_index_in_dim(begins_all, replica_index, 0, keepdims=False)
    my_begin = jnp.sum(jnp.where(is_mine, own_begins, 0))
    my_length = jnp.sum(jnp.where(is_mine, own_lengths, 0))
    columns = jnp.arange(COLS, dtype=jnp.int32)
    offset = columns - my_begin
    inside = (offset >= 0) & (offset < my_length)
    picked = jnp.take(grad_out, jnp.clip(offset, 0, slot_width - 1), axis=1)
    spread = jnp.where(inside[None, :], picked, jnp.zeros_like(picked)).reshape(
        token_count, shards, block_width
    )
    received = lax.all_to_all(spread, "tp", split_axis=1, concat_axis=1, tiled=True)
    grad_block = jnp.sum(received, axis=1)
    grad_columns = lax.dot_general(
        lax.all_gather(tokens, "tp", axis=1, tiled=True),
        grad_block,
        (((0,), (0,)), ((), ())),
        preferred_element_type=jnp.float32,
    )
    summed = lax.psum_scatter(
        grad_columns.astype(jnp.bfloat16), "rep", scatter_dimension=0, tiled=True
    ).astype(jnp.float32)
    new_master, new_first, new_second = adam_update(master, first, second, summed)
    weights = new_master.astype(jnp.bfloat16)
    healthy = lax.all_gather(weights, "rep", axis=0, tiled=True)
    replica_rows = lax.all_gather(weights, "tp", axis=1, tiled=True)
    slot_begins = jnp.sum(jnp.where(is_mine[None, :], begins_all, 0), axis=1)
    slot_lengths = jnp.sum(jnp.where(is_mine[None, :], lengths, 0), axis=1)
    within = jnp.arange(slot_width, dtype=jnp.int32)
    source_cols = slot_begins[:, None] + within[None, :]
    valid = within[None, :] < slot_lengths[:, None]
    taken = jnp.take(replica_rows, jnp.clip(source_cols, 0, COLS - 1).reshape(-1), axis=1)
    outgoing = jnp.where(valid.reshape(-1)[None, :], taken, jnp.zeros_like(taken))
    outgoing = outgoing.reshape(replica_rows.shape[0], replicas, slot_width)
    arrived = lax.all_to_all(outgoing, "rep", split_axis=1, concat_axis=0, tiled=True)
    slot_weights = arrived.reshape(1, -1, slot_width)
    return (new_master, new_first, new_second, healthy, slot_weights)


def solution(mesh):
    placed = (P("rep", "tp"), P("rep", "tp"), P(), P("rep", "tp"), P("rep", "tp"), P("rep", "tp"))
    return jax.shard_map(
        on_device,
        mesh=mesh,
        in_specs=placed,
        out_specs=(
            P("rep", "tp"),
            P("rep", "tp"),
            P("rep", "tp"),
            P(None, "tp"),
            P("rep", None, "tp"),
        ),
        check_vma=False,
    )
```

profile of v0, /device:TPU:0, one launch (start us, length us, event | category | flops | bytes accessed | tf_op | source)
XLA Modules:
  0.0 925.4 jit_solution(10204115507527925698)
XLA Ops:
  7.2 0.0 copy-start.2
  7.2 0.0 all-gather.4.cloned.1.call-start
  7.2 0.7 all-gather.4.cloned.1.call-update
  7.9 0.0 reduce-scatter.2.cloned.1.call-start
  8.0 0.0 copy-done.2
  8.0 0.2 dynamic-slice_reduce_fusion
  8.2 0.1 select_reduce_fusion.1
  8.3 0.2 dynamic-slice_reduce_fusion.1
  8.5 2.9 copy.32
  11.3 0.6 select_reduce_fusion.2
  12.0 0.7 compare_select_fusion.2
  12.7 9.6 %gather_fusion = bf16[2048,1024]{1,0:T(8,128)(2,1)} fusion(bf16[1024,1024]{0,1:T(8,128)(2,1)S(1)} %copy.32, s32[2048]{0:T(1024)S(1)} %broadcast_clamp_fusion.1), kind=kCustom, calls=%fused_computation | custom fusion | bytes 8396800 | tf_op jit(solution)/shard_map/jit(_take)/gather | solution.py:44
  22.3 0.7 compare_and_fusion
  22.9 1.3 fusion.9
  24.3 3.1 select_select_fusion.1
  27.4 98.3 %all_to_all.20 = bf16[1024,4,512]{0,2,1:T(8,128)(2,1)} all-to-all(bf16[1024,4,512]{0,2,1:T(8,128)(2,1)S(1)} %select_select_fusion.1), channel_id=1, replica_groups=mesh['rep'=8,'tp'=4] {'tp'}, dimensions={1} | all-to-all | bytes 8388608 | tf_op jit(solution)/shard_map/all_to_all | solution.py:48
  125.7 3.3 reduce_sum.50
  129.0 34.2 %all-gather.4.cloned.1.call-done = bf16[1024,8192]{1,0:T(8,128)(2,1)} async-done(((bf16[1024,2048]{1,0:T(8,128)(2,1)}), bf16[1024,8192]{1,0:T(8,128)(2,1)}) %all-gather.4.cloned.1.call-update) | async-done | bytes 16777232 | tf_op jit(solution)/shard_map/all_gather | solution.py:51
  163.1 16.8 %fusion = bf16[8192,512]{0,1:T(8,128)(2,1)} fusion(bf16[1024,512]{0,1:T(8,128)(2,1)S(1)} %reduce_sum.50, bf16[1024,8192]{1,0:T(8,128)(2,1)} %all-gather.4.cloned.1.call-done), kind=kOutput, calls=%fused_computation.4 | convolution fusion | flops 8594128896 | bytes 26214400 | tf_op jit(solution)/shard_map/dot_general | solution.py:50
  179.9 0.0 copy-start
  179.9 0.0 reduce-scatter.2.cloned.1.call-update
  179.9 0.0 all-gather.8.cloned.1.call-start
  180.0 1.5 copy-done
  181.5 1.8 copy.31
  183.3 0.0 copy-start.1
  183.3 3.0 copy.33
  186.3 0.0 copy-done.1
  186.3 1.8 copy.35
  188.2 139.8 %reduce-scatter.2.cloned.1.call-done = bf16[1024,512]{0,1:T(8,128)(2,1)} async-done(((bf16[8192,512]{0,1:T(8,128)(2,1)}), bf16[1024,512]{0,1:T(8,128)(2,1)}) %reduce-scatter.2.cloned.1.call-update) | async-done | bytes 1048592 | tf_op jit(solution)/shard_map/reduce_scatter | solution.py:56
  328.0 7.5 fusion.10
  335.5 0.0 all-gather.8.cloned.1.call-update
  335.5 0.1 fusion.3
  335.6 0.1 iota_compare_fusion
  335.8 33.4 %all-gather.8.cloned.1.call-done = bf16[1024,2048]{0,1:T(8,128)(2,1)} async-done(((bf16[1024,512]{0,1:T(8,128)(2,1)}), bf16[1024,2048]{0,1:T(8,128)(2,1)}) %all-gather.8.cloned.1.call-update) | async-done | bytes 4194320 | tf_op jit(solution)/shard_map/all_gather | solution.py:62
  369.2 43.2 %gather_fusion.1 = bf16[8192,1024]{1,0:T(8,128)(2,1)} fusion(bf16[1024,2048]{0,1:T(8,128)(2,1)} %all-gather.8.cloned.1.call-done, s32[8192]{0:T(1024)S(1)} %broadcast_clamp_fusion), kind=kCustom, calls=%fused_computation.1 | custom fusion | bytes 33587200 | tf_op jit(solution)/shard_map/jit(_take)/gather | solution.py:68
  412.4 14.6 %select_select_fusion = bf16[1024,8,1024]{0,2,1:T(8,128)(2,1)} fusion(bf16[1024,8,1024]{0,2,1:T(8,128)(2,1)} %bitcast.21, pred[8,1024]{1,0:T(8,128)(4,1)S(1)} %get-tuple-element.30, pred[8,1024]{1,0:T(8,128)(4,1)S(1)} %get-tuple-element.29), kind=kLoop, calls=%fused_computation.2 | loop fusion | flops 16777216 | bytes 33570816 | tf_op jit(solution)/shard_map/jit(_where)/select_n | solution.py:69
  427.0 5.8 all-to-all-start.1
  432.7 0.0 all-gather.6.cloned.1.call-start
  432.8 0.5 all-gather.6.cloned.1.call-update
  433.3 2.9 copy.37
  436.2 2.9 copy.38
  439.1 1.8 copy.39
  440.9 402.1 %all-gather.6.cloned.1.call-done = bf16[8192,512]{0,1:T(8,128)(2,1)} async-done(((bf16[1024,512]{0,1:T(8,128)(2,1)}), bf16[8192,512]{0,1:T(8,128)(2,1)}) %all-gather.6.cloned.1.call-update) | async-done | bytes 8388624 | tf_op jit(solution)/shard_map/all_gather | solution.py:61
  843.0 11.9 %copy.40 = bf16[8192,512]{1,0:T(8,128)(2,1)} copy(bf16[8192,512]{0,1:T(8,128)(2,1)} %all-gather.6.cloned.1.call-done) | data formatting | bytes 16777216
  855.0 42.4 %all-to-all-done.1 = bf16[1024,8,1024]{0,2,1:T(8,128)(2,1)} async-done(((bf16[1024,8,1024]{0,2,1:T(8,128)(2,1)}), bf16[1024,8,1024]{0,2,1:T(8,128)(2,1)}, u32[]{:S(2)}, u32[]{:S(2)}) %all-to-all-start.1) | async-done | bytes 16777248 | tf_op jit(solution)/shard_map/all_to_all | solution.py:71
  897.4 21.5 %copy.36 = bf16[8,1024,1,1024]{3,1,0,2:T(8,128)(2,1)} copy(bf16[8,1024,1,1024]{1,3,0,2:T(8,128)(2,1)} %bitcast.8) | data formatting | bytes 33554432 | tf_op jit(solution)/shard_map/all_to_all | solution.py:71
  (6 shorter events, 0.1 us)
Async XLA Ops:
  7.2 0.8 copy-start.2
  7.2 156.0 %all-gather.4.cloned.1.call-start = ((), (), s32[]{:S(2)}) async-start(), calls=%async_computation.3 | async-start | bytes 20971520 | tf_op jit(solution)/shard_map/all_gather | solution.py:51
  7.9 320.1 %reduce-scatter.2.cloned.1.call-start = ((), (), s32[]{:S(2)}) async-start(), calls=%async_computation.4 | async-start | bytes 9437184 | tf_op jit(solution)/shard_map/reduce_scatter | solution.py:56
  179.9 1.6 copy-start
  179.9 189.3 %all-gather.8.cloned.1.call-start = ((), (), s32[]{:S(2)}) async-start(), calls=%async_computation.6 | async-start | bytes 5242880 | tf_op jit(solution)/shard_map/all_gather | solution.py:62
  183.3 3.0 copy-start.1
  427.0 470.4 %all-to-all-start.1 = ((bf16[1024,8,1024]{0,2,1:T(8,128)(2,1)}), bf16[1024,8,1024]{0,2,1:T(8,128)(2,1)}, u32[]{:S(2)}, u32[]{:S(2)}) async-start(bf16[1024,8,1024]{0,2,1:T(8,128)(2,1)} %select_select_fusion), calls=%async_computation.2 | async-start | bytes 33554432 | tf_op jit(solution)/shard_map/all_to_all | solution.py:71
  432.7 410.3 %all-gather.6.cloned.1.call-start = ((), (), s32[]{:S(2)}) async-start(), calls=%async_computation.5 | async-start | bytes 9437184 | tf_op jit(solution)/shard_map/all_gather | solution.py:61
Sparse Core Ops, SparseCore 0:
  9.5 153.5 all-gather.3
  180.1 147.8 reduce-scatter.1
  335.6 33.5 all-gather.7
  435.4 407.5 all-gather.5
where the time goes:
time: 927 us; the launch traced here: 925 us
  waiting for transfers between devices  653 us (70%)
  local copies, waits for them, and re-layouts  105 us (11%)
  blocking collectives  98.3 us (11%)
  other arithmetic  32.1 us (3%)
  matrix products  16.8 us (2%)
  between operations  13.9 us (1%)
    all_gather x1, waiting for transfers between devices, on_device(): healthy = lax.all_gather(weights, 'rep', axis=0, tiled=True)  402 us
    reduce_scatter x1, waiting for transfers between devices, on_device(): lax.psum_scatter(grad_columns.astype(jnp.bfloat16), 'rep', scatter_dimens...  140 us
    all_to_all x1, blocking collectives, on_device(): lax.all_to_all(spread, 'tp', split_axis=1, concat_axis=1, tiled=True)  98.3 us
    gather x1, local copies, waits for them, and re-layouts, on_device(): jnp.take(replica_rows, jnp.clip(source_cols, 0, COLS - 1).reshape(-1), ax...  43.2 us
    all_to_all x1, waiting for transfers between devices, on_device(): lax.all_to_all(outgoing, 'rep', split_axis=1, concat_axis=0, tiled=True)  42.4 us
    all_gather x1, waiting for transfers between devices, on_device(): lax.all_gather(tokens, 'tp', axis=1, tiled=True)  34.2 us
    all_gather x1, waiting for transfers between devices, on_device(): replica_rows = lax.all_gather(weights, 'tp', axis=1, tiled=True)  33.4 us
    unnamed x15, local copies, waits for them, and re-layouts  30.6 us
  transfers between devices with their start and end apart: 5, of which 5 were waited for; matrix products, arithmetic and copies ran while one was open for 5% of the time, Pallas kernels for 0%

commit v1 on v0

--- a/solution.py
+++ b/solution.py
@@ -1,6 +1,8 @@
 import jax
 import jax.numpy as jnp
 from jax import lax
+from jax.experimental import pallas as pl
+from jax.experimental.pallas import tpu as pltpu
 from jax.sharding import PartitionSpec as P
 
 COLS = 2048
@@ -24,7 +26,7 @@
     return (new_master, new_first, new_second)
 
 
-def on_device(tokens, grad_out, lengths, master, first, second):
+def on_device_general(tokens, grad_out, lengths, master, first, second):
     shards = lax.axis_size("tp")
     replicas = lax.axis_size("rep")
     column_index = lax.axis_index("tp")
@@ -73,10 +75,128 @@
     return (new_master, new_first, new_second, healthy, slot_weights)
 
 
+def unit_tables(lengths, unit, slot_units, total_units):
+    shards = lax.axis_size("tp")
+    begins_all = jnp.cumsum(lengths, axis=1) - lengths
+    own_lengths = lax.dynamic_index_in_dim(lengths, lax.axis_index("rep"), 0, keepdims=False) // unit
+    own_begins = lax.dynamic_index_in_dim(begins_all, lax.axis_index("rep"), 0, keepdims=False) // unit
+    column = jnp.arange(total_units, dtype=jnp.int32)[:, None]
+    inside = (own_begins[None, :] <= column) & (column < (own_begins + own_lengths)[None, :])
+    place = jnp.arange(shards, dtype=jnp.int32)[None, :] * slot_units + column - own_begins[None, :]
+    source = jnp.sum(jnp.where(inside, place, 0), axis=1)
+    mine = jnp.arange(shards, dtype=jnp.int32) == lax.axis_index("tp")
+    my_begin = jnp.sum(jnp.where(mine, own_begins, 0))
+    my_length = jnp.sum(jnp.where(mine, own_lengths, 0))
+    within = jnp.arange(slot_units, dtype=jnp.int32)
+    slot_unit = jnp.clip(my_begin + within, 0, total_units - 1)
+    valid = (within < my_length).astype(jnp.int32)
+    me = jnp.full((1,), lax.axis_index("tp"), jnp.int32)
+    return source.astype(jnp.int32), jnp.concatenate([slot_unit, valid, me]).astype(jnp.int32)
+
+
+def partial_product(source, tokens, slots, unit, block_width):
+    rows, features = tokens.shape
+    per_block = block_width // unit
+    slot_units = slots.shape[2] // unit
+    blocks = source.shape[0] // per_block
+    tile = min(512, features)
+
+    def body(source_ref, tokens_ref, *refs):
+        out_ref = refs[-1]
+        for p in range(per_block):
+            out_ref[0, :, p * unit : (p + 1) * unit] = lax.dot_general(
+                tokens_ref[...], refs[p][0], (((0,), (0,)), ((), ())), preferred_element_type=jnp.float32
+            ).astype(out_ref.dtype)
+
+    def unit_spec(p):
+        def index(j, f, source_ref):
+            at = source_ref[j * per_block + p]
+            return (at // slot_units, 0, at % slot_units)
+
+        return pl.BlockSpec((1, rows, unit), index)
+
+    return pl.pallas_call(
+        body,
+        out_shape=jax.ShapeDtypeStruct((blocks, features, block_width), jnp.bfloat16),
+        grid_spec=pltpu.PrefetchScalarGridSpec(
+            num_scalar_prefetch=1,
+            grid=(blocks, features // tile),
+            in_specs=[pl.BlockSpec((rows, tile), lambda j, f, s: (0, f))] + [unit_spec(p) for p in range(per_block)],
+            out_specs=pl.BlockSpec((1, tile, block_width), lambda j, f, s: (j, f, 0)),
+        ),
+    )(source, tokens, *([slots] * per_block))
+
+
+def place_weights(table, blocks, unit, slot_units, replicas, shards):
+    _, rows, block_width = blocks.shape
+    per_block = block_width // unit
+
+    def body(table_ref, own_ref, *refs):
+        healthy_ref, slot_ref = refs[-2:]
+        healthy_ref[...] = own_ref[0]
+        for s in range(slot_units):
+            keep = table_ref[slot_units + s] > 0
+            value = refs[s][0]
+            slot_ref[0, :, s * unit : (s + 1) * unit] = jnp.where(keep, value, jnp.zeros_like(value))
+
+    def unit_spec(s):
+        def index(r, table_ref):
+            at = table_ref[s]
+            return (r * shards + at // per_block, 0, at % per_block)
+
+        return pl.BlockSpec((1, rows, unit), index)
+
+    return pl.pallas_call(
+        body,
+        out_shape=(
+            jax.ShapeDtypeStruct((replicas * rows, block_width), blocks.dtype),
+            jax.ShapeDtypeStruct((1, replicas * rows, slot_units * unit), blocks.dtype),
+        ),
+        grid_spec=pltpu.PrefetchScalarGridSpec(
+            num_scalar_prefetch=1,
+            grid=(replicas,),
+            in_specs=[pl.BlockSpec((1, rows, block_width), lambda r, t: (r * shards + t[2 * slot_units], 0, 0))]
+            + [unit_spec(s) for s in range(slot_units)],
+            out_specs=(
+                pl.BlockSpec((rows, block_width), lambda r, t: (r, 0)),
+                pl.BlockSpec((1, rows, slot_units * unit), lambda r, t: (0, r, 0)),
+            ),
+        ),
+    )(table, *([blocks] * (slot_units + 1)))
+
+
+def on_device(tokens, grad_out, lengths, master, first, second):
+    shards = lax.axis_size("tp")
+    replicas = lax.axis_size("rep")
+    rows, block_width = master.shape
+    unit = COLS // (2 * shards)
+    slot_units = grad_out.shape[1] // unit
+    row_blocks = replicas // shards
+    source, table = unit_tables(lengths, unit, slot_units, COLS // unit)
+    slots = lax.all_gather(grad_out, "tp")
+    partial = partial_product(source, tokens, slots, unit, block_width)
+    chunk = lax.psum_scatter(
+        partial.reshape(replicas * rows, block_width), "rep", scatter_dimension=0, tiled=True
+    )
+    moves = [
+        (k * shards + j, (row_blocks * j + k % row_blocks) * shards + k // row_blocks)
+        for k in range(replicas)
+        for j in range(shards)
+    ]
+    summed = lax.ppermute(chunk, ("rep", "tp"), moves).astype(jnp.float32)
+    new_master, new_first, new_second = adam_update(master, first, second, summed)
+    weights = new_master.astype(jnp.bfloat16)
+    blocks = lax.all_gather(weights, ("rep", "tp"))
+    healthy, slot_weights = place_weights(table, blocks, unit, slot_units, replicas, shards)
+    return (new_master, new_first, new_second, healthy, slot_weights)
+
+
 def solution(mesh):
     placed = (P("rep", "tp"), P("rep", "tp"), P(), P("rep", "tp"), P("rep", "tp"), P("rep", "tp"))
+    shards, replicas = mesh.shape["tp"], mesh.shape["rep"]
+    by_units = (COLS // (2 * shards)) % 128 == 0 and replicas % shards == 0
     return jax.shard_map(
-        on_device,
+        on_device if by_units else on_device_general,
         mesh=mesh,
         in_specs=placed,
         out_specs=(

time: 927 us -> 516 us (0.56)
  waiting for transfers between devices: 653 us -> 449 us
  local copies, waits for them, and re-layouts: 105 us -> 0.01 us
  blocking collectives: 98.3 us -> 0 us
  Pallas kernels: 0 us -> 40.3 us
  other arithmetic: 32.1 us -> 9.99 us
  matrix products: 16.8 us -> 0 us
    all_gather x3 -> x2, waiting for transfers between devices: 470 us -> 300 us  [the longest x1 239 us: on_device(): blocks = lax.all_gather(weights, ('rep', 'tp'))]
    all_to_all x1 -> x0, blocking collectives: 98.3 us -> none  [on_device(): lax.all_to_all(spread, 'tp', split_axis=1, concat_axis=1, tiled=True)]
    gather x2 -> x0, local copies, waits for them, and re-layouts: 52.8 us -> none  [the longest x1 43.2 us: on_device(): jnp.take(replica_rows, jnp.clip(source_cols, 0, COLS - 1).reshape(-1), ax...]
    all_to_all x1 -> x0, waiting for transfers between devices: 42.4 us -> none  [on_device(): lax.all_to_all(outgoing, 'rep', split_axis=1, concat_axis=0, tiled=True)]
    pallas_call x0 -> x2, Pallas kernels: none -> 40.3 us  [the longest x1 21 us: partial_product(): pl.pallas_call(body, out_shape=jax.ShapeDtypeStruct((blocks, features, bl...]
    unnamed x15 -> x4, local copies, waits for them, and re-layouts: 30.6 us -> 0.01 us
    all_to_all x1 -> x0, local copies, waits for them, and re-layouts: 21.5 us -> none  [on_device(): lax.all_to_all(outgoing, 'rep', split_axis=1, concat_axis=0, tiled=True)]
    select_n x4 -> x0, other arithmetic: 18.4 us -> none  [the longest x1 14.6 us: on_device(): jnp.where(valid.reshape(-1)[None, :], taken, jnp.zeros_like(taken))]
  transfers between devices with their start and end apart: 5 -> 4, of which waited for: 5 -> 3; matrix products, arithmetic and copies ran while one was open for 5% -> 1% of each run, Pallas kernels for 0% -> 0%
where the time goes in v1:
time: 516 us; the launch traced here: 515 us
  waiting for transfers between devices  449 us (87%)
  Pallas kernels  40.3 us (8%)
  between operations  13.8 us (3%)
  other arithmetic  9.99 us (2%)
    all_gather x1, waiting for transfers between devices, on_device(): blocks = lax.all_gather(weights, ('rep', 'tp'))  239 us
    reduce_scatter x1, waiting for transfers between devices, on_device(): lax.psum_scatter(partial.reshape(replicas * rows, block_width), 'rep', sc...  148 us
    all_gather x1, waiting for transfers between devices, on_device(): slots = lax.all_gather(grad_out, 'tp')  61.5 us
    pallas_call x1, Pallas kernels, partial_product(): pl.pallas_call(body, out_shape=jax.ShapeDtypeStruct((blocks, features, bl...  21 us
    pallas_call x1, Pallas kernels, place_weights(): pl.pallas_call(body, out_shape=(jax.ShapeDtypeStruct((replicas * rows, bl...  19.3 us
  transfers between devices with their start and end apart: 4, of which 3 were waited for; matrix products, arithmetic and copies ran while one was open for 1% of the time, Pallas kernels for 0%

profile of v1, /device:TPU:0, one launch (start us, length us, event | category | flops | bytes accessed | tf_op | source)
XLA Modules:
  0.0 515.0 jit_solution(5551686531672748408)
XLA Ops:
  7.2 0.0 copy-start.1
  7.2 0.0 all-gather.5.cloned.1.call-start
  7.2 0.7 all-gather.5.cloned.1.call-update
  7.9 0.0 reduce-scatter.2.cloned.1.call-start
  8.0 0.0 copy-done.1
  8.0 0.2 dynamic-slice_reduce_fusion.1
  8.2 0.2 dynamic-slice_reduce_fusion
  8.4 0.6 select_reduce_fusion.source_ref
  9.0 61.5 %all-gather.5.cloned.1.call-done = bf16[4096,1024]{1,0:T(8,128)(2,1)} async-done(((bf16[1024,1024]{1,0:T(8,128)(2,1)}), bf16[4096,1024]{1,0:T(8,128)(2,1)}) %all-gather.5.cloned.1.call-update) | async-done | bytes 8388624 | tf_op jit(solution)/shard_map/all_gather | solution.py:176
  70.6 21.0 %shard_map.101 = bf16[4,2048,512]{2,1,0:T(8,128)(2,1)} custom-call(s32[8]{0:T(128)} %select_reduce_fusion.source_ref, bf16[1024,2048]{1,0:T(8,128)(2,1)} %tokens_ref.1, bf16[4,1024,1024]{2,1,0:T(8,128)(2,1)} %bitcast.10, bf16[4,1024,1024]{2,1,0:T(8,128)(2,1)} %bitcast.11), custom_call_target="tpu_custom_call" | custom-call | tf_op jit(solution)/shard_map/pallas_call | solution.py:118
  91.6 0.0 copy-start
  91.6 0.0 reduce-scatter.2.cloned.1.call-update
  91.6 0.0 all-gather.7.cloned.1.call-start
  91.7 148.0 %reduce-scatter.2.cloned.1.call-done = bf16[1024,512]{1,0:T(8,128)(2,1)} async-done(((bf16[8192,512]{1,0:T(8,128)(2,1)}), bf16[1024,512]{1,0:T(8,128)(2,1)}) %reduce-scatter.2.cloned.1.call-update) | async-done | bytes 1048592 | tf_op jit(solution)/shard_map/reduce_scatter | solution.py:178
  239.7 1.9 collective-permute-start
  241.5 0.0 collective-permute-done
  241.5 0.0 copy-done
  241.5 6.3 %fusion.11 = (bf16[1024,512]{1,0:T(8,128)(2,1)}, f32[1024,512]{1,0:T(8,128)}, f32[1024,512]{1,0:T(8,128)}, f32[1024,512]{1,0:T(8,128)}) fusion(f32[1024,512]{1,0:T(8,128)S(1)} %copy-done, bf16[1024,512]{1,0:T(8,128)(2,1)S(1)} %collective-permute-done, f32[1024,512]{1,0:T(8,128)} %param.11, f32[1024,512]{1,0:T(8,128)} %param.10), kind=kLoop, calls=%fused_computation.43 | loop fusion | flops 8388608 | bytes 14680064 | tf_op jit(solution)/shard_map/convert_element_type | solution.py:188
  247.8 0.0 all-gather.7.cloned.1.call-update
  247.8 0.7 fusion.9
  248.6 0.7 add_clamp_fusion
  249.2 0.6 compare_convert_fusion
  249.8 0.7 pad_add_fusion.table_ref
  250.5 238.7 %all-gather.7.cloned.1.call-done = bf16[32768,512]{1,0:T(8,128)(2,1)} async-done(((bf16[1024,512]{1,0:T(8,128)(2,1)}), bf16[32768,512]{1,0:T(8,128)(2,1)}) %all-gather.7.cloned.1.call-update) | async-done | bytes 33554448 | tf_op jit(solution)/shard_map/all_gather | solution.py:189
  489.2 19.3 %shard_map.102 = (bf16[8192,512]{1,0:T(8,128)(2,1)}, bf16[1,8192,1024]{2,1,0:T(8,128)(2,1)}) custom-call(s32[9]{0:T(128)} %pad_add_fusion.table_ref, bf16[32,1024,512]{2,1,0:T(8,128)(2,1)} %bitcast.4, bf16[32,1024,512]{2,1,0:T(8,128)(2,1)} %bitcast.5, bf16[32,1024,512]{2,1,0:T(8,128)(2,1)} %bitcast.6, bf16[32,1024,512]{2,1,0:T(8,128)(2,1)} %bitcast.7, ...), custom_call_target="tpu_custom_call" | custom-call | tf_op jit(solution)/shard_map/pallas_call | solution.py:149
  (3 shorter events, 0.0 us)
Async XLA Ops:
  7.2 0.8 copy-start.1
  7.2 63.4 %all-gather.5.cloned.1.call-start = ((), (), s32[]{:S(2)}) async-start(), calls=%async_computation.2 | async-start | bytes 10485760 | tf_op jit(solution)/shard_map/all_gather | solution.py:176
  7.9 231.8 %reduce-scatter.2.cloned.1.call-start = ((), (), s32[]{:S(2)}) async-start(), calls=%async_computation.1 | async-start | bytes 9437184 | tf_op jit(solution)/shard_map/reduce_scatter | solution.py:178
  91.6 149.9 %copy-start = (f32[1024,512]{1,0:T(8,128)S(1)}, f32[1024,512]{1,0:T(8,128)}, u32[]{:S(2)}) copy-start(f32[1024,512]{1,0:T(8,128)} %param.9) | copy-start | bytes 6291460
  91.6 397.6 %all-gather.7.cloned.1.call-start = ((), (), s32[]{:S(2)}) async-start(), calls=%async_computation.3 | async-start | bytes 34603008 | tf_op jit(solution)/shard_map/all_gather | solution.py:189
  239.7 1.9 collective-permute-start
Sparse Core Ops, SparseCore 0:
  9.5 60.9 all-gather.4
  91.7 147.8 reduce-scatter.1
  248.0 241.1 all-gather.6

commit v2 on v1

--- a/solution.py
+++ b/solution.py
@@ -1,3 +1,5 @@
+import functools
+
 import jax
 import jax.numpy as jnp
 from jax import lax
@@ -14,6 +16,7 @@
 learning_rate = 0.02
 weight_decay = 0.1
 epsilon = 1e-08
+MESH = pl.DeviceIdType.MESH
 
 
 def adam_update(master, first, second, gradient):
@@ -165,6 +168,169 @@
     )(table, *([blocks] * (slot_units + 1)))
 
 
+def gather_kernel(halves, shards, chunks, own_ref, all_ref, local_sem, send_sem, recv_sem):
+    rep, tp = lax.axis_index("rep"), lax.axis_index("tp")
+    c, x, y, z = tp % 2, tp // 2, rep % 2, rep // 2
+    step_y, step_x = 1 - 2 * y, 2 * (1 - 2 * x)
+    here = (rep, tp)
+    side = (rep + (1 - c) * step_y, tp + c * step_x)
+    cross = (rep + c * step_y, tp + (1 - c) * step_x)
+    far = (rep + step_y, tp + step_x)
+    mate = (rep, tp + 1 - 2 * c)
+    above, below = (rep + 2, tp), (rep - 2, tp)
+    rows = own_ref.shape[0] // chunks
+
+    barrier = pltpu.get_barrier_semaphore()
+    for at in (side, cross, mate):
+        pl.semaphore_signal(barrier, inc=1, device_id=at, device_id_type=MESH)
+
+    @pl.when(z < halves - 1)
+    def _():
+        pl.semaphore_signal(barrier, inc=1, device_id=above, device_id_type=MESH)
+
+    @pl.when(z > 0)
+    def _():
+        pl.semaphore_signal(barrier, inc=1, device_id=below, device_id_type=MESH)
+
+    pl.semaphore_wait(barrier, 3 + jnp.minimum(z, 1) + jnp.minimum(halves - 1 - z, 1))
+
+    spots = [(0, 0)] + [(w, d) for w in range(1, halves) for d in (-1, 1)]
+    number = {spot: n for n, spot in enumerate(spots)}
+
+    def place(col, spot, h):
+        w, d = spot
+        return all_ref.at[(col[0] + 2 * w * d) * shards + col[1], pl.ds(h * rows, rows)]
+
+    def copy(kind, spot, col, h, to, out=None, mine=False):
+        out = kind if out is None else out
+        at = place(col, spot, h)
+        seen = spot
+        if kind == 0:
+            seen = out_spot(spot, out)
+        return pltpu.make_async_remote_copy(
+            src_ref=own_ref.at[pl.ds(h * rows, rows)] if mine else at,
+            dst_ref=at,
+            send_sem=send_sem.at[out, number[spot], h],
+            recv_sem=recv_sem.at[kind, number[seen], h],
+            device_id=to,
+            device_id_type=MESH,
+        )
+
+    def out_spot(spot, out):
+        w, d = spot
+        return (w + 1, -1 if out == 0 else 1)
+
+    def line_sends(spot, h):
+        w, d = spot
+        mine = w == 0
+        sends = [
+            (None, copy(1, spot, here, h, side, mine=mine)),
+            (None, copy(2, spot, here, h, cross, mine=mine)),
+            (None, copy(4, spot, here, h, mate, mine=mine)),
+        ]
+        if w < halves - 1:
+            if d <= 0:
+                sends.insert(0, (z < halves - 1, copy(0, spot, here, h, above, out=0, mine=mine)))
+            if d >= 0:
+                sends.insert(0, (z > 0, copy(0, spot, here, h, below, out=8, mine=mine)))
+        return sends
+
+    def side_sends(spot, h):
+        return [(None, copy(3, spot, side, h, cross)), (None, copy(5, spot, side, h, mate))]
+
+    def cross_sends(spot, h):
+        return [(None, copy(6, spot, cross, h, mate))]
+
+    def far_sends(spot, h):
+        return [(None, copy(7, spot, far, h, mate))]
+
+    def arrival(kind, spot, col, h):
+        at = place(col, spot, h)
+        return pltpu.make_async_remote_copy(
+            src_ref=at,
+            dst_ref=at,
+            send_sem=send_sem.at[0, 0, 0],
+            recv_sem=recv_sem.at[kind, number[spot], h],
+            device_id=mate,
+            device_id_type=MESH,
+        )
+
+    def exists(spot):
+        w, d = spot
+        if w == 0:
+            return None
+        return z >= w if d < 0 else z < halves - w
+
+    def guarded(condition, act):
+        if condition is None:
+            act()
+        else:
+            pl.when(condition)(act)
+
+    def act_on(kind, spot, col, sends):
+        def act():
+            for h in range(chunks):
+                if not (kind == 0 and spot[0] == 0):
+                    arrival(kind, spot, col, h).wait_recv()
+                for condition, send in sends(spot, h):
+                    guarded(condition, send.start)
+
+        guarded(exists(spot), act)
+
+    keep = pltpu.make_async_copy(own_ref, all_ref.at[rep * shards + tp], local_sem)
+    for wave in range(halves + 2):
+        for spot in spots:
+            if spot[0] == wave:
+                act_on(0, spot, here, line_sends)
+        if wave == 0:
+            keep.start()
+        for spot in spots:
+            if spot[0] == wave - 1:
+                act_on(1, spot, side, side_sends)
+                act_on(2, spot, cross, cross_sends)
+        for spot in spots:
+            if spot[0] == wave - 2:
+                act_on(3, spot, far, far_sends)
+
+    def finish(spot):
+        def act():
+            for h in range(chunks):
+                for kind, col in ((4, (rep, tp + 1 - 2 * c)), (5, None), (6, None), (7, None)):
+                    if kind == 5:
+                        col = (rep + c * step_y, tp + 1 - 2 * c + (1 - c) * step_x)
+                    if kind == 6:
+                        col = (rep + (1 - c) * step_y, tp + 1 - 2 * c + c * step_x)
+                    if kind == 7:
+                        col = (rep + step_y, tp + 1 - 2 * c + step_x)
+                    arrival(kind, spot, col, h).wait_recv()
+                for sends in (line_sends, side_sends, cross_sends, far_sends):
+                    for condition, send in sends(spot, h):
+                        guarded(condition, send.wait_send)
+
+        guarded(exists(spot), act)
+
+    for spot in spots:
+        finish(spot)
+    keep.wait()
+
+
+def gather_blocks(weights, shards, replicas, chunks=2):
+    halves = replicas // 2
+    spots = 2 * halves - 1
+    return pl.pallas_call(
+        functools.partial(gather_kernel, halves, shards, chunks),
+        out_shape=jax.ShapeDtypeStruct((replicas * shards,) + weights.shape, weights.dtype),
+        in_specs=[pl.BlockSpec(memory_space=pl.ANY)],
+        out_specs=pl.BlockSpec(memory_space=pl.ANY),
+        scratch_shapes=[
+            pltpu.SemaphoreType.DMA,
+            pltpu.SemaphoreType.DMA((9, spots, chunks)),
+            pltpu.SemaphoreType.DMA((8, spots, chunks)),
+        ],
+        compiler_params=pltpu.CompilerParams(collective_id=0, has_side_effects=True),
+    )(weights)
+
+
 def on_device(tokens, grad_out, lengths, master, first, second):
     shards = lax.axis_size("tp")
     replicas = lax.axis_size("rep")
@@ -186,7 +352,7 @@
     summed = lax.ppermute(chunk, ("rep", "tp"), moves).astype(jnp.float32)
     new_master, new_first, new_second = adam_update(master, first, second, summed)
     weights = new_master.astype(jnp.bfloat16)
-    blocks = lax.all_gather(weights, ("rep", "tp"))
+    blocks = gather_blocks(weights, shards, replicas)
     healthy, slot_weights = place_weights(table, blocks, unit, slot_units, replicas, shards)
     return (new_master, new_first, new_second, healthy, slot_weights)
 
@@ -194,7 +360,7 @@
 def solution(mesh):
     placed = (P("rep", "tp"), P("rep", "tp"), P(), P("rep", "tp"), P("rep", "tp"), P("rep", "tp"))
     shards, replicas = mesh.shape["tp"], mesh.shape["rep"]
-    by_units = (COLS // (2 * shards)) % 128 == 0 and replicas % shards == 0
+    by_units = (COLS // (2 * shards)) % 128 == 0 and replicas % shards == 0 and shards == 4 and replicas % 2 == 0
     return jax.shard_map(
         on_device if by_units else on_device_general,
         mesh=mesh,

time: 516 us -> 466 us (0.903)
  waiting for transfers between devices: 449 us -> 210 us
  Pallas kernels: 40.3 us -> 229 us
    all_gather x1 -> x0, waiting for transfers between devices: 239 us -> none  [on_device(): blocks = lax.all_gather(weights, ('rep', 'tp'))]
    pallas_call x0 -> x1, Pallas kernels: none -> 188 us  [gather_blocks(): pl.pallas_call(functools.partial(gather_kernel, halves, shards, chunks),...]
  transfers between devices with their start and end apart: 4 -> 3, of which waited for: 3 -> 2; matrix products, arithmetic and copies ran while one was open for 1% -> 1% of each run, Pallas kernels for 0% -> 0%
where the time goes in v2:
time: 466 us; the launch traced here: 465 us
  Pallas kernels  229 us (49%)
  waiting for transfers between devices  210 us (45%)
  between operations  14.1 us (3%)
  other arithmetic  9.99 us (2%)
    pallas_call x1, Pallas kernels, gather_blocks(): pl.pallas_call(functools.partial(gather_kernel, halves, shards, chunks),...  188 us
    reduce_scatter x1, waiting for transfers between devices, on_device(): lax.psum_scatter(partial.reshape(replicas * rows, block_width), 'rep', sc...  148 us
    all_gather x1, waiting for transfers between devices, on_device(): slots = lax.all_gather(grad_out, 'tp')  61.5 us
    pallas_call x1, Pallas kernels, partial_product(): pl.pallas_call(body, out_shape=jax.ShapeDtypeStruct((blocks, features, bl...  21 us
    pallas_call x1, Pallas kernels, place_weights(): pl.pallas_call(body, out_shape=(jax.ShapeDtypeStruct((replicas * rows, bl...  19.2 us
  transfers between devices with their start and end apart: 3, of which 2 were waited for; matrix products, arithmetic and copies ran while one was open for 1% of the time, Pallas kernels for 0%

profile of v2, /device:TPU:0, one launch (start us, length us, event | category | flops | bytes accessed | tf_op | source)
XLA Modules:
  0.0 465.0 jit_solution(913160747620272110)
XLA Ops:
  7.2 0.0 copy-start.1
  7.2 0.0 all-gather.3.cloned.1.call-start
  7.2 0.7 all-gather.3.cloned.1.call-update
  7.9 0.0 reduce-scatter.2.cloned.1.call-start
  8.0 0.0 copy-done.1
  8.0 0.2 dynamic-slice_reduce_fusion.1
  8.2 0.2 dynamic-slice_reduce_fusion
  8.4 0.6 select_reduce_fusion.source_ref
  9.0 61.5 %all-gather.3.cloned.1.call-done = bf16[4096,1024]{1,0:T(8,128)(2,1)} async-done(((bf16[1024,1024]{1,0:T(8,128)(2,1)}), bf16[4096,1024]{1,0:T(8,128)(2,1)}) %all-gather.3.cloned.1.call-update) | async-done | bytes 8388624 | tf_op jit(solution)/shard_map/all_gather | solution.py:342
  70.6 21.0 %shard_map.101 = bf16[4,2048,512]{2,1,0:T(8,128)(2,1)} custom-call(s32[8]{0:T(128)} %select_reduce_fusion.source_ref, bf16[1024,2048]{1,0:T(8,128)(2,1)} %tokens_ref.1, bf16[4,1024,1024]{2,1,0:T(8,128)(2,1)} %bitcast.4, bf16[4,1024,1024]{2,1,0:T(8,128)(2,1)} %bitcast.5), custom_call_target="tpu_custom_call" | custom-call | tf_op jit(solution)/shard_map/pallas_call | solution.py:121
  91.6 0.0 copy-start
  91.6 0.0 reduce-scatter.2.cloned.1.call-update
  91.6 148.0 %reduce-scatter.2.cloned.1.call-done = bf16[1024,512]{1,0:T(8,128)(2,1)} async-done(((bf16[8192,512]{1,0:T(8,128)(2,1)}), bf16[1024,512]{1,0:T(8,128)(2,1)}) %reduce-scatter.2.cloned.1.call-update) | async-done | bytes 1048592 | tf_op jit(solution)/shard_map/reduce_scatter | solution.py:344
  239.7 1.9 collective-permute-start
  241.5 0.6 fusion.9
  242.2 0.6 add_clamp_fusion
  242.8 0.7 compare_convert_fusion
  243.5 0.7 pad_add_fusion.table_ref
  244.1 0.0 collective-permute-done
  244.2 0.0 copy-done
  244.2 6.3 %fusion.11 = (bf16[1024,512]{1,0:T(8,128)(2,1)}, f32[1024,512]{1,0:T(8,128)}, f32[1024,512]{1,0:T(8,128)}, f32[1024,512]{1,0:T(8,128)}) fusion(f32[1024,512]{1,0:T(8,128)S(1)} %copy-done, bf16[1024,512]{1,0:T(8,128)(2,1)S(1)} %collective-permute-done, f32[1024,512]{1,0:T(8,128)} %param.11, f32[1024,512]{1,0:T(8,128)} %param.10), kind=kLoop, calls=%fused_computation.43 | loop fusion | flops 8388608 | bytes 14680064 | tf_op jit(solution)/shard_map/convert_element_type | solution.py:354
  250.5 188.4 %shard_map.102.own_ref.refs_0_.refs_1_.refs_2_.refs_3_ = bf16[32,1024,512]{2,1,0:T(8,128)(2,1)} custom-call(bf16[1024,512]{1,0:T(8,128)(2,1)} %get-tuple-element.12.own_ref), custom_call_target="tpu_custom_call" | custom-call | tf_op jit(solution)/shard_map/pallas_call | solution.py:320
  438.9 19.2 %shard_map.103 = (bf16[8192,512]{1,0:T(8,128)(2,1)}, bf16[1,8192,1024]{2,1,0:T(8,128)(2,1)}) custom-call(s32[9]{0:T(128)} %pad_add_fusion.table_ref, bf16[32,1024,512]{2,1,0:T(8,128)(2,1)} %shard_map.102.own_ref.refs_0_.refs_1_.refs_2_.refs_3_, bf16[32,1024,512]{2,1,0:T(8,128)(2,1)} %shard_map.102.own_ref.refs_0_.refs_1_.refs_2_.refs_3_, ...), custom_call_target="tpu_custom_call" | custom-call | tf_op jit(solution)/shard_map/pallas_call | solution.py:152
  (3 shorter events, 0.0 us)
Async XLA Ops:
  7.2 0.8 copy-start.1
  7.2 63.4 %all-gather.3.cloned.1.call-start = ((), (), s32[]{:S(2)}) async-start(), calls=%async_computation.2 | async-start | bytes 10485760 | tf_op jit(solution)/shard_map/all_gather | solution.py:342
  7.9 231.8 %reduce-scatter.2.cloned.1.call-start = ((), (), s32[]{:S(2)}) async-start(), calls=%async_computation.1 | async-start | bytes 9437184 | tf_op jit(solution)/shard_map/reduce_scatter | solution.py:344
  91.6 152.6 %copy-start = (f32[1024,512]{1,0:T(8,128)S(1)}, f32[1024,512]{1,0:T(8,128)}, u32[]{:S(2)}) copy-start(f32[1024,512]{1,0:T(8,128)} %param.9) | copy-start | bytes 6291460
  239.7 4.5 collective-permute-start
Sparse Core Ops, SparseCore 0:
  9.5 60.9 all-gather.2
  91.7 147.8 reduce-scatter.1

commit v3 on v2

--- a/solution.py
+++ b/solution.py
@@ -340,12 +340,15 @@
     row_blocks = replicas // shards
     source, table = unit_tables(lengths, unit, slot_units, COLS // unit)
     slots = lax.all_gather(grad_out, "tp")
+    order = [(q % 2) * (shards // 2) + q // 2 for q in range(shards)]
+    by_block = source.reshape(shards, -1)
+    source = jnp.concatenate([by_block[q] for q in order])
     partial = partial_product(source, tokens, slots, unit, block_width)
     chunk = lax.psum_scatter(
         partial.reshape(replicas * rows, block_width), "rep", scatter_dimension=0, tiled=True
     )
     moves = [
-        (k * shards + j, (row_blocks * j + k % row_blocks) * shards + k // row_blocks)
+        (k * shards + j, (row_blocks * j + k % row_blocks) * shards + order[k // row_blocks])
         for k in range(replicas)
         for j in range(shards)
     ]

time: 466 us -> 463 us (level)
  no operation moved by 1% of the time
where the time goes in v3:
time: 463 us
  Pallas kernels  227 us (49%)
  waiting for transfers between devices  210 us (45%)
  between operations  14.1 us (3%)
  other arithmetic  10 us (2%)
    pallas_call x1, Pallas kernels, gather_blocks(): pl.pallas_call(functools.partial(gather_kernel, halves, shards, chunks),...  186 us
    reduce_scatter x1, waiting for transfers between devices, on_device(): lax.psum_scatter(partial.reshape(replicas * rows, block_width), 'rep', sc...  148 us
    all_gather x1, waiting for transfers between devices, on_device(): slots = lax.all_gather(grad_out, 'tp')  61.4 us
    pallas_call x1, Pallas kernels, partial_product(): pl.pallas_call(body, out_shape=jax.ShapeDtypeStruct((blocks, features, bl...  21 us
    pallas_call x1, Pallas kernels, place_weights(): pl.pallas_call(body, out_shape=(jax.ShapeDtypeStruct((replicas * rows, bl...  19.3 us
  transfers between devices with their start and end apart: 3, of which 2 were waited for; matrix products, arithmetic and copies ran while one was open for 1% of the time, Pallas kernels for 0%

profile of v3, /device:TPU:0, one launch (start us, length us, event | category | flops | bytes accessed | tf_op | source)
XLA Modules:
  0.0 462.9 jit_solution(18039203256010714293)
XLA Ops:
  7.2 0.0 copy-start.1
  7.2 0.0 all-gather.3.cloned.1.call-start
  7.2 0.7 all-gather.3.cloned.1.call-update
  7.9 0.0 reduce-scatter.2.cloned.1.call-start
  8.0 0.0 copy-done.1
  8.0 0.2 dynamic-slice_reduce_fusion.1
  8.2 0.2 dynamic-slice_reduce_fusion
  8.4 0.1 select_reduce_fusion
  8.5 0.1 fusion.14
  8.6 0.6 pad_add_fusion.source_ref
  9.2 61.4 %all-gather.3.cloned.1.call-done = bf16[4096,1024]{1,0:T(8,128)(2,1)} async-done(((bf16[1024,1024]{1,0:T(8,128)(2,1)}), bf16[4096,1024]{1,0:T(8,128)(2,1)}) %all-gather.3.cloned.1.call-update) | async-done | bytes 8388624 | tf_op jit(solution)/shard_map/all_gather | solution.py:342
  70.6 21.0 %shard_map.101 = bf16[4,2048,512]{2,1,0:T(8,128)(2,1)} custom-call(s32[8]{0:T(128)} %pad_add_fusion.source_ref, bf16[1024,2048]{1,0:T(8,128)(2,1)} %tokens_ref.1, bf16[4,1024,1024]{2,1,0:T(8,128)(2,1)} %bitcast.4, bf16[4,1024,1024]{2,1,0:T(8,128)(2,1)} %bitcast.5), custom_call_target="tpu_custom_call" | custom-call | tf_op jit(solution)/shard_map/pallas_call | solution.py:121
  91.6 0.0 copy-start
  91.6 0.0 reduce-scatter.2.cloned.1.call-update
  91.6 148.0 %reduce-scatter.2.cloned.1.call-done = bf16[1024,512]{1,0:T(8,128)(2,1)} async-done(((bf16[8192,512]{1,0:T(8,128)(2,1)}), bf16[1024,512]{1,0:T(8,128)(2,1)}) %reduce-scatter.2.cloned.1.call-update) | async-done | bytes 1048592 | tf_op jit(solution)/shard_map/reduce_scatter | solution.py:347
  239.7 1.9 collective-permute-start
  241.5 0.6 fusion.9
  242.2 0.6 add_clamp_fusion
  242.8 0.7 compare_convert_fusion
  243.5 0.7 pad_add_fusion.1.table_ref
  244.1 0.0 collective-permute-done
  244.2 0.0 copy-done
  244.2 6.3 %fusion.11 = (bf16[1024,512]{1,0:T(8,128)(2,1)}, f32[1024,512]{1,0:T(8,128)}, f32[1024,512]{1,0:T(8,128)}, f32[1024,512]{1,0:T(8,128)}) fusion(f32[1024,512]{1,0:T(8,128)S(1)} %copy-done, bf16[1024,512]{1,0:T(8,128)(2,1)S(1)} %collective-permute-done, f32[1024,512]{1,0:T(8,128)} %param.11, f32[1024,512]{1,0:T(8,128)} %param.10), kind=kLoop, calls=%fused_computation.44 | loop fusion | flops 8388608 | bytes 14680064 | tf_op jit(solution)/shard_map/convert_element_type | solution.py:357
  250.4 186.3 %shard_map.102.own_ref.refs_0_.refs_1_.refs_2_.refs_3_ = bf16[32,1024,512]{2,1,0:T(8,128)(2,1)} custom-call(bf16[1024,512]{1,0:T(8,128)(2,1)} %get-tuple-element.12.own_ref), custom_call_target="tpu_custom_call" | custom-call | tf_op jit(solution)/shard_map/pallas_call | solution.py:320
  436.8 19.3 %shard_map.103 = (bf16[8192,512]{1,0:T(8,128)(2,1)}, bf16[1,8192,1024]{2,1,0:T(8,128)(2,1)}) custom-call(s32[9]{0:T(128)} %pad_add_fusion.1.table_ref, bf16[32,1024,512]{2,1,0:T(8,128)(2,1)} %shard_map.102.own_ref.refs_0_.refs_1_.refs_2_.refs_3_, bf16[32,1024,512]{2,1,0:T(8,128)(2,1)} %shard_map.102.own_ref.refs_0_.refs_1_.refs_2_.refs_3_, ...), custom_call_target="tpu_custom_call" | custom-call | tf_op jit(solution)/shard_map/pallas_call | solution.py:152
  (3 shorter events, 0.0 us)
Async XLA Ops:
  7.2 0.8 copy-start.1
  7.2 63.4 %all-gather.3.cloned.1.call-start = ((), (), s32[]{:S(2)}) async-start(), calls=%async_computation.2 | async-start | bytes 10485760 | tf_op jit(solution)/shard_map/all_gather | solution.py:342
  7.9 231.8 %reduce-scatter.2.cloned.1.call-start = ((), (), s32[]{:S(2)}) async-start(), calls=%async_computation.1 | async-start | bytes 9437184 | tf_op jit(solution)/shard_map/reduce_scatter | solution.py:347
  91.6 152.6 %copy-start = (f32[1024,512]{1,0:T(8,128)S(1)}, f32[1024,512]{1,0:T(8,128)}, u32[]{:S(2)}) copy-start(f32[1024,512]{1,0:T(8,128)} %param.9) | copy-start | bytes 6291460
  239.7 4.5 collective-permute-start
Sparse Core Ops, SparseCore 0:
  9.5 60.9 all-gather.2
  91.7 147.8 reduce-scatter.1
